TPU v7x, 32 devices: a whole 2x2x4 slice. The times are simulated.
32 devices in a mesh: dp: 8 (over y, x, core), tensor: 4 (over z).
Axes of the slice: x: 2, y: 2, z: 4, core: 2. Of those that a mesh axis runs over, the one named last changes fastest.
Arguments:
- tokens: bfloat16 [4096, 768], P('dp'), may hold values from -6 to 6
- lengths: int32 [8, 16], P('dp'), may hold values from 0 to 512, as said below
- w_query: bfloat16 [768, 768], P(None, 'tensor'), may hold values from -0.21875 to 0.21875
- w_key: bfloat16 [768, 768], P(None, 'tensor'), may hold values from -0.21875 to 0.21875
- w_value: bfloat16 [768, 768], P(None, 'tensor'), may hold values from -0.21875 to 0.21875
- b_query: float32 [768], P('tensor'), may hold values from -3 to 3
- b_value: float32 [768], P('tensor'), may hold values from -3 to 3
- w_out: bfloat16 [768, 768], P('tensor'), may hold values from -0.625 to 0.625
- b_out: float32 [768], replicated, may hold values from -3 to 3
- g_attn: float32 [768], replicated, may hold values from 0.5 to 1.5
- b_attn: float32 [768], replicated, may hold values from -3 to 3
- w_up: bfloat16 [768, 3072], P(None, 'tensor'), may hold values from -0.21875 to 0.21875
- b_up: float32 [3072], P('tensor'), may hold values from -3 to 3
- w_down: bfloat16 [3072, 768], P('tensor'), may hold values from -0.109375 to 0.109375
- b_down: float32 [768], replicated, may hold values from -3 to 3
- g_ffn: float32 [768], replicated, may hold values from 0.5 to 1.5
- b_ffn: float32 [768], replicated, may hold values from -3 to 3
- out_grad: bfloat16 [4096, 768], P('dp'), may hold values from -6 to 6
- pool_grad: float32 [128, 1728], P('dp'), may hold values from -6 to 6
Outputs:
- layer_out: bfloat16 [4096, 768], P('dp')
- pools: float32 [128, 1728], replicated
- d_tokens: float32 [4096, 768], P('dp')
- d_w_query: float32 [768, 768], P(None, 'tensor')
- d_w_key: float32 [768, 768], P(None, 'tensor')
- d_w_value: float32 [768, 768], P(None, 'tensor')
- d_b_query: float32 [768], P('tensor')
- d_b_value: float32 [768], P('tensor')
- d_w_out: float32 [768, 768], P('tensor')
- d_b_out: float32 [768], replicated
- d_g_attn: float32 [768], replicated
- d_b_attn: float32 [768], replicated
- d_w_up: float32 [768, 3072], P(None, 'tensor')
- d_b_up: float32 [3072], P('tensor')
- d_w_down: float32 [3072, 768], P('tensor')
- d_b_down: float32 [768], replicated
- d_g_ffn: float32 [768], replicated
- d_b_ffn: float32 [768], replicated
Inputs may be any that keep to these rules, and one draw needn't show every extreme that they name: In each bucket the nonzero lengths come first and add up to at most 512; the first is nonzero; in every draw some bucket holds one sentence of exactly 512 tokens.
All inputs are finite; a program needn't handle non-finite values.
Results may differ from a plain program's by a relative error of at most 0.013.
Values sent between devices are 32-bit elements; how exact they have to be, the bound alone decides.
No kernel may reach another device: no remote copies, remote signals or barrier semaphores. Data moves between devices by JAX's collectives and lax.ppermute only.
A program may use at most 128 MiB of HBM per device.

v0:
```python
import jax
import jax.numpy as jnp
from jax import lax
from jax.sharding import PartitionSpec as P

HDIM = 64
SENTS = 16
norm_eps = 1e-06
pool_eps = 1e-05
highest = lax.Precision.HIGHEST


def truncations(width):
    return [width, width * 2 // 3, width // 3, width // 6, width // 12]


def segment_ids(sizes, slot_count):
    ends = jnp.cumsum(sizes, dtype=jnp.int32)
    places = jnp.arange(slot_count, dtype=jnp.int32)
    return jnp.sum((places[:, None] >= ends[None, :]).astype(jnp.int32), axis=1)


def norm_stats(rows):
    centre = jnp.mean(rows, axis=-1, keepdims=True)
    shifted = rows - centre
    inverse = lax.rsqrt(jnp.mean(shifted * shifted, axis=-1, keepdims=True) + norm_eps)
    return (shifted * inverse, inverse)


def norm_back(grad_in, normal, inverse):
    centre = jnp.mean(grad_in, axis=-1, keepdims=True)
    along = jnp.mean(grad_in * normal, axis=-1, keepdims=True)
    return inverse * (grad_in - centre - normal * along)


def gelu_exact(upper):
    return jax.nn.gelu(upper, approximate=False)


def attention_scores(query_heads, key_heads, allowed, score_scale):
    scores = (
        jnp.einsum("qhd,khd->hqk", query_heads, key_heads, preferred_element_type=jnp.float32)
        * score_scale
    )
    return jnp.where(allowed[None], scores, -1000000000.0)


def shards(
    tokens,
    lengths,
    w_query,
    w_key,
    w_value,
    b_query,
    b_value,
    w_out,
    b_out,
    g_attn,
    b_attn,
    w_up,
    b_up,
    w_down,
    b_down,
    g_ffn,
    b_ffn,
    out_grad,
    pool_grad,
):
    slot_count = tokens.shape[0]
    model_width = tokens.shape[1]
    local_cols = w_query.shape[1]
    head_count = local_cols // HDIM
    score_scale = HDIM ** (-0.5)
    segment = segment_ids(lengths[0], slot_count)
    allowed = segment[:, None] == segment[None, :]
    inputs = tokens.astype(jnp.float32)
    query_rows = (jnp.dot(tokens, w_query, preferred_element_type=jnp.float32) + b_query).astype(
        jnp.bfloat16
    )
    key_rows = jnp.dot(tokens, w_key, preferred_element_type=jnp.float32).astype(jnp.bfloat16)
    value_rows = (jnp.dot(tokens, w_value, preferred_element_type=jnp.float32) + b_value).astype(
        jnp.bfloat16
    )
    query_heads = query_rows.reshape(slot_count, head_count, HDIM)
    key_heads = key_rows.reshape(slot_count, head_count, HDIM)
    value_heads = value_rows.reshape(slot_count, head_count, HDIM)
    scores = attention_scores(query_heads, key_heads, allowed, score_scale)
    top_score = jnp.max(scores, axis=-1, keepdims=True)
    log_total = top_score + jnp.log(jnp.sum(jnp.exp(scores - top_score), axis=-1, keepdims=True))
    probs_low = jnp.exp(scores - log_total).astype(jnp.bfloat16)
    mixed = jnp.einsum("hqk,khd->qhd", probs_low, value_heads, preferred_element_type=jnp.float32)
    mixed = mixed.reshape(slot_count, local_cols).astype(jnp.bfloat16)
    partial_value = jnp.dot(mixed, w_out, preferred_element_type=jnp.float32)
    attn_total = lax.psum(partial_value, "tensor")
    normal_attn, inverse_attn = norm_stats(inputs + attn_total + b_out)
    normed = normal_attn * g_attn + b_attn
    normed_low = normed.astype(jnp.bfloat16)
    upper = jnp.dot(normed_low, w_up, preferred_element_type=jnp.float32) + b_up
    act_rows = gelu_exact(upper).astype(jnp.bfloat16)
    down_total = lax.psum(jnp.dot(act_rows, w_down, preferred_element_type=jnp.float32), "tensor")
    normal_ffn, inverse_ffn = norm_stats(normed + down_total + b_down)
    final = normal_ffn * g_ffn + b_ffn
    layer_out = final.astype(jnp.bfloat16)
    sentence = jnp.arange(SENTS, dtype=jnp.int32)
    member = (segment[None, :] == sentence[:, None]).astype(jnp.float32)
    denom = jnp.maximum(lengths[0], 1).astype(jnp.float32)[:, None]
    pooled = jnp.dot(member, final, precision=highest, preferred_element_type=jnp.float32) / denom
    pieces = []
    factors = []
    for keep_width in truncations(model_width):
        leading = pooled[:, :keep_width]
        factor = lax.rsqrt(jnp.mean(leading * leading, axis=1, keepdims=True) + pool_eps)
        pieces.append(leading * factor)
        factors.append(factor)
    pools = lax.all_gather(jnp.concatenate(pieces, axis=1), "dp", axis=0, tiled=True)
    d_pooled = jnp.zeros_like(pooled)
    offset = 0
    for keep_width, factor in zip(truncations(model_width), factors):
        leading = pooled[:, :keep_width]
        upstream = pool_grad[:, offset : offset + keep_width]
        inner = jnp.mean(upstream * leading, axis=1, keepdims=True)
        d_pooled = d_pooled.at[:, :keep_width].add(factor * upstream - leading * factor**3 * inner)
        offset = offset + keep_width
    spread_back = jnp.einsum(
        "st,sd->td", member, d_pooled / denom, precision=highest, preferred_element_type=jnp.float32
    )
    d_final = out_grad.astype(jnp.float32) + spread_back
    g_ffn_part = jnp.sum(d_final * normal_ffn, axis=0)
    b_ffn_part = jnp.sum(d_final, axis=0)
    d_resid = norm_back(d_final * g_ffn, normal_ffn, inverse_ffn)
    b_down_part = jnp.sum(d_resid, axis=0)
    resid_low = d_resid.astype(jnp.bfloat16)
    w_down_part = jnp.einsum("tf,td->fd", act_rows, resid_low, preferred_element_type=jnp.float32)
    d_act = jnp.einsum("td,fd->tf", resid_low, w_down, preferred_element_type=jnp.float32)
    d_upper = jax.vjp(gelu_exact, upper)[1](d_act)[0]
    b_up_part = jnp.sum(d_upper, axis=0)
    upper_low = d_upper.astype(jnp.bfloat16)
    w_up_part = jnp.einsum("td,tf->df", normed_low, upper_low, preferred_element_type=jnp.float32)
    normed_term = jnp.einsum("tf,df->td", upper_low, w_up, preferred_element_type=jnp.float32)
    d_normed = d_resid + lax.psum(normed_term, "tensor")
    g_attn_part = jnp.sum(d_normed * normal_attn, axis=0)
    b_attn_part = jnp.sum(d_normed, axis=0)
    d_hidden = norm_back(d_normed * g_attn, normal_attn, inverse_attn)
    b_out_part = jnp.sum(d_hidden, axis=0)
    hidden_low = d_hidden.astype(jnp.bfloat16)
    w_out_part = jnp.einsum("tc,td->cd", mixed, hidden_low, preferred_element_type=jnp.float32)
    d_mixed = jnp.einsum("td,cd->tc", hidden_low, w_out, preferred_element_type=jnp.float32)
    d_mixed = d_mixed.astype(jnp.bfloat16).reshape(slot_count, head_count, HDIM)
    scores_again = attention_scores(query_heads, key_heads, allowed, score_scale)
    probs = jnp.exp(scores_again - log_total)
    probs_again = probs.astype(jnp.bfloat16)
    d_probs = jnp.einsum("qhd,khd->hqk", d_mixed, value_heads, preferred_element_type=jnp.float32)
    row_inner = jnp.sum(probs * d_probs, axis=-1, keepdims=True)
    d_scores = (probs * (d_probs - row_inner) * score_scale).astype(jnp.bfloat16)
    d_query = jnp.einsum(
        "hqk,khd->qhd", d_scores, key_heads, preferred_element_type=jnp.float32
    ).reshape(slot_count, local_cols)
    d_key = jnp.einsum(
        "hqk,qhd->khd", d_scores, query_heads, preferred_element_type=jnp.float32
    ).reshape(slot_count, local_cols)
    d_value = jnp.einsum(
        "hqk,qhd->khd", probs_again, d_mixed, preferred_element_type=jnp.float32
    ).reshape(slot_count, local_cols)
    b_query_part = jnp.sum(d_query, axis=0)
    b_value_part = jnp.sum(d_value, axis=0)
    query_low = d_query.astype(jnp.bfloat16)
    key_low = d_key.astype(jnp.bfloat16)
    value_low = d_value.astype(jnp.bfloat16)
    w_query_part = jnp.einsum("td,tc->dc", tokens, query_low, preferred_element_type=jnp.float32)
    w_key_part = jnp.einsum("td,tc->dc", tokens, key_low, preferred_element_type=jnp.float32)
    w_value_part = jnp.einsum("td,tc->dc", tokens, value_low, preferred_element_type=jnp.float32)
    input_term = jnp.einsum("tc,dc->td", query_low, w_query, preferred_element_type=jnp.float32)
    input_term = input_term + jnp.einsum(
        "tc,dc->td", key_low, w_key, preferred_element_type=jnp.float32
    )
    input_term = input_term + jnp.einsum(
        "tc,dc->td", value_low, w_value, preferred_element_type=jnp.float32
    )
    d_tokens = d_hidden + lax.psum(input_term, "tensor")
    grad_sums = lax.psum(
        (
            w_query_part,
            w_key_part,
            w_value_part,
            b_query_part,
            b_value_part,
            w_out_part,
            b_out_part,
            g_attn_part,
            b_attn_part,
            w_up_part,
            b_up_part,
            w_down_part,
            b_down_part,
            g_ffn_part,
            b_ffn_part,
        ),
        "dp",
    )
    (
        d_w_query,
        d_w_key,
        d_w_value,
        d_b_query,
        d_b_value,
        d_w_out,
        d_b_out,
        d_g_attn,
        d_b_attn,
        d_w_up,
        d_b_up,
        d_w_down,
        d_b_down,
        d_g_ffn,
        d_b_ffn,
    ) = grad_sums
    return (
        layer_out,
        pools,
        d_tokens,
        d_w_query,
        d_w_key,
        d_w_value,
        d_b_query,
        d_b_value,
        d_w_out,
        d_b_out,
        d_g_attn,
        d_b_attn,
        d_w_up,
        d_b_up,
        d_w_down,
        d_b_down,
        d_g_ffn,
        d_b_ffn,
    )


def solution(mesh):
    return jax.shard_map(
        shards,
        mesh=mesh,
        in_specs=(
            P("dp", None),
            P("dp", None),
            P(None, "tensor"),
            P(None, "tensor"),
            P(None, "tensor"),
            P("tensor"),
            P("tensor"),
            P("tensor", None),
            P(),
            P(),
            P(),
            P(None, "tensor"),
            P("tensor"),
            P("tensor", None),
            P(),
            P(),
            P(),
            P("dp", None),
            P("dp", None),
        ),
        out_specs=(
            P("dp", None),
            P(),
            P("dp", None),
            P(None, "tensor"),
            P(None, "tensor"),
            P(None, "tensor"),
            P("tensor"),
            P("tensor"),
            P("tensor", None),
            P(),
            P(),
            P(),
            P(None, "tensor"),
            P("tensor"),
            P("tensor", None),
            P(),
            P(),
            P(),
        ),
        check_vma=False,
    )
```

profile of v0, /device:TPU:0, one launch (start us, length us, event | category | flops | bytes accessed | tf_op | source)
XLA Modules:
  0.0 486.1 jit_solution(11460330406638272772)
XLA Ops:
  7.3 0.9 copy.49
  8.6 1.7 convolution_convert_fusion.2
  13.3 1.0 convolution_convert_fusion
  14.3 1.6 fusion.70
  16.0 71.8 %all-reduce.8.cloned.1.call-done = f32[512,768]{1,0:T(8,128)} async-done(((f32[512,768]{1,0:T(8,128)}), f32[512,768]{1,0:T(8,128)}) %all-reduce.8.cloned.1.call-update) | async-done | bytes 1572880 | tf_op jit(solution)/shard_map/psum | solution.py:94
  87.7 1.7 fusion.64
  90.2 5.4 %multiply_convert_fusion.1 = (bf16[512,768]{1,0:T(8,128)(2,1)S(1)}, f32[512,768]{1,0:T(8,128)}, f32[512,768]{1,0:T(8,128)}) fusion(f32[768]{0:T(1024)S(1)} %copy-done.59, bf16[768,768]{1,0:T(8,128)(2,1)S(1)} %copy-done, f32[512,768]{1,0:T(8,128)S(1)} %get-tuple-element.189, f32[768]{0:T(1024)S(1)} %copy-done.53, f32[768]{0:T(1024)S(1)} %copy-done.35, ...), kind=kOutput, calls=%fused_computation.24 | convolution fusion | flops 631898112 | bytes 6697984 | tf_op jit(solution)/shard_map/dot_general | solution.py:98
  95.5 0.9 copy-done.16
  96.4 1.9 fusion.71
  99.9 1.2 convert_bitcast_fusion
  101.0 65.6 %all-reduce.10.cloned.1.call-done = f32[512,768]{1,0:T(8,128)} async-done(((f32[512,768]{1,0:T(8,128)}), f32[512,768]{1,0:T(8,128)}) %all-reduce.10.cloned.1.call-update) | async-done | bytes 1572880 | tf_op jit(solution)/shard_map/psum | solution.py:100
  166.7 2.0 fusion.62
  169.7 1.0 multiply_reduce_fusion.9
  173.5 1.3 add_select_fusion.2
  175.5 1.4 scatter-add.19
  177.0 3.9 multiply_reduce_fusion.1
  181.0 1.5 fusion.60
  183.5 1.8 fusion.69
  185.3 0.9 copy-done.63
  186.2 2.0 fusion.42
  188.4 68.0 %all-reduce.12.cloned.1.call-done = f32[512,768]{1,0:T(8,128)} async-done(((f32[512,768]{1,0:T(8,128)}), f32[512,768]{1,0:T(8,128)}) %all-reduce.12.cloned.1.call-update) | async-done | bytes 1572880 | tf_op jit(solution)/shard_map/psum | solution.py:140
  256.4 3.3 multiply_reduce_fusion.2
  259.8 1.1 fusion.61
  260.9 1.1 copy-done.2
  262.5 2.3 fusion.72
  264.8 7.5 %fusion.66 = (f32[3,64]{1,0:T(4,128)}, bf16[512,3,64]{0,2,1:T(8,128)(2,1)S(1)}) fusion(bf16[512,3,64]{0,2,1:T(8,128)(2,1)S(1)} %bitcast.68, f32[3,512,512]{1,2,0:T(8,128)} %fusion.72, f32[3,512]{1,0:T(4,128)S(1)} %copy-done.44, f32[3,512,512]{1,2,0:T(8,128)} %copy-done.8, pred[512,512]{0,1:T(8,128)(4,1)S(1)} %copy-done.12), kind=kOutput, calls=%fused_computation.151 | convolution fusion | flops 109512512 | bytes 6953728 | tf_op jit(solution)/shard_map/hqk,khd->qhd/dot_general | solution.py:155
  272.3 6.9 %fusion.27 = bf16[3,64,512]{2,1,0:T(8,128)(2,1)S(1)} fusion(bf16[512,3,64]{0,2,1:T(8,128)(2,1)} %bitcast.78, f32[3,512,512]{1,2,0:T(8,128)} %fusion.72, f32[3,512,512]{1,2,0:T(8,128)} %copy-done.8, f32[3,512]{1,0:T(4,128)S(1)} %copy-done.44, pred[512,512]{0,1:T(8,128)(4,1)S(1)} %copy-done.12), kind=kOutput, calls=%fused_computation.60 | convolution fusion | flops 109414400 | bytes 6952960 | tf_op jit(solution)/shard_map/hqk,qhd->khd/dot_general | solution.py:158
  279.3 3.6 fusion.65
  284.2 1.6 add_add_fusion
  285.9 3.9 fusion.44
  289.8 2.4 fusion.40
  292.2 1.1 convolution_bitcast_fusion.2
  293.4 1.1 convolution_bitcast_fusion.1
  294.5 1.1 convolution_bitcast_fusion
  295.7 1.1 fusion.37
  297.7 10.6 %all_gather.3 = f32[128,1728]{1,0:T(8,128)S(1)} all-gather(f32[16,1728]{1,0:T(8,128)S(1)} %copy-done.30), channel_id=1, replica_groups=mesh['dp'=8,'tensor'=4] {'dp'}, dimensions={0}, use_global_device_ids=true | all-gather | bytes 995328 | tf_op jit(solution)/shard_map/all_gather | solution.py:115
  308.3 1.2 copy.54
  309.7 25.0 %all-reduce = (f32[192]{0:T(256)}, f32[192]{0:T(256)}, f32[768]{0:T(1024)}, f32[768]{0:T(1024)}, f32[768]{0:T(1024)}, /*index=5*/f32[768]{0:T(1024)}, f32[768]{0:T(1024)}, f32[768]{0:T(1024)}, f32[768]{0:T(1024)}) all-reduce(f32[192]{0:T(256)S(1)} %reduce_sum.296, ...), channel_id=1, replica_groups=mesh['dp'=8,'tensor'=4] {'dp'}, use_global_device_ids=true, to_apply=%region_35.36 | all-reduce | flops 5760 | bytes 46080 | tf_op jit(solution)/shard_map/psum | solution.py:180
  334.7 19.3 %all-reduce.14.cloned.1.call-done = f32[512,768]{1,0:T(8,128)} async-done(((f32[512,768]{1,0:T(8,128)}), f32[512,768]{1,0:T(8,128)}) %all-reduce.14.cloned.1.call-update) | async-done | bytes 1572880 | tf_op jit(solution)/shard_map/psum | solution.py:179
  354.1 2.7 add.261
  356.8 114.3 %all-reduce.16.cloned.1.call-done = (f32[768,192]{0,1:T(8,128)}, f32[768,192]{0,1:T(8,128)}, f32[768,192]{0,1:T(8,128)}, f32[192,768]{1,0:T(8,128)}, f32[768,768]{1,0:T(8,128)}, /*index=5*/f32[768,768]{1,0:T(8,128)}) async-done(((f32[768,192]{0,1:T(8,128)}, f32[768,192]{0,1:T(8,128)}, f32[768,192]{0,1:T(8,128)}, f32[192,768]{1,0:T(8,128)}, f32[768,768]{1,0:T(8,128)}, /*index=5*/f32[768,768]{1,0:T(8,128)}), ...) | async-done | bytes 7077904 | tf_op jit(solution)/shard_map/psum | solution.py:180
  471.1 2.0 copy.77
  473.2 0.8 copy.78
  474.0 0.8 copy.79
  474.8 0.8 copy.80
  475.6 1.4 copy.81
  477.0 1.1 copy-done.9
  478.1 1.4 copy.82
  (179 shorter events, 14.3 us)
Async XLA Ops:
  7.2 82.6 %copy-start = (bf16[768,768]{1,0:T(8,128)(2,1)S(1)}, bf16[768,768]{1,0:T(8,128)(2,1)}, u32[]{:S(2)}) copy-start(bf16[768,768]{1,0:T(8,128)(2,1)} %param.42) | copy-start | bytes 3538948
  7.2 3.1 copy-start.4
  7.2 3.1 copy-start.26
  7.2 3.1 copy-start.60
  7.2 80.5 %all-reduce.8.cloned.1.call-start = ((), (), s32[]{:S(2)}) async-start(), calls=%async_computation | async-start | bytes 3145728 | tf_op jit(solution)/shard_map/psum | solution.py:94
  8.6 4.6 copy-start.11
  11.6 1.7 copy-start.8
  14.3 73.4 %copy-start.52 = (f32[768]{0:T(1024)S(1)}, f32[768]{0:T(1024)}, u32[]{:S(2)}) copy-start(f32[768]{0:T(1024)} %param.39) | copy-start | bytes 9220
  15.9 150.8 %all-reduce.10.cloned.1.call-start = ((), (), s32[]{:S(2)}) async-start(), calls=%async_computation.1 | async-start | bytes 3145728 | tf_op jit(solution)/shard_map/psum | solution.py:100
  90.1 6.3 %copy-start.57 = (bf16[768,768]{1,0:T(8,128)(2,1)S(1)}, bf16[768,768]{1,0:T(8,128)(2,1)}, u32[]{:S(2)}) copy-start(bf16[768,768]{1,0:T(8,128)(2,1)} %param.44) | copy-start | bytes 3538948
  98.4 158.1 %all-reduce.12.cloned.1.call-start = ((), (), s32[]{:S(2)}) async-start(), calls=%async_computation.2 | async-start | bytes 3145728 | tf_op jit(solution)/shard_map/psum | solution.py:140
  168.6 2.1 copy-start.5
  168.7 2.0 copy-start.36
  169.7 5.9 %copy-start.41 = (f32[512]{0:T(512)}, f32[512]{0:T(512)S(1)}, u32[]{:S(2)}) copy-start(f32[512]{0:T(512)S(1)} %add_rsqrt_fusion) | copy-start | bytes 6148
  173.5 2.0 copy-start.34
  176.9 4.0 copy-start.6
  176.9 4.0 copy-start.37
  176.9 4.0 copy-start.42
  176.9 4.0 copy-start.46
  176.9 4.0 copy-start.48
  180.9 2.0 copy-start.65
  180.9 2.6 copy-start.66
  182.5 2.8 copy-start.7
  188.2 165.9 %all-reduce.14.cloned.1.call-start = ((), (), s32[]{:S(2)}) async-start(), calls=%async_computation.3 | async-start | bytes 3145728 | tf_op jit(solution)/shard_map/psum | solution.py:179
  259.8 2.2 copy-start.15
  262.4 2.4 copy-start.12
  262.5 2.3 copy-start.20
  262.5 2.3 copy-start.44
  279.3 3.6 copy-start.27
  285.8 4.0 copy-start.54
  285.8 185.3 %all-reduce.16.cloned.1.call-start = ((), (), s32[]{:S(2)}) async-start(), calls=%async_computation.4 | async-start | bytes 14155776 | tf_op jit(solution)/shard_map/psum | solution.py:180
  285.9 3.9 copy-start.64
  293.4 2.3 copy-start.3
  293.4 2.3 copy-start.18
  296.8 12.7 %copy-start.55 = (f32[3,64]{1,0:T(4,128)S(1)}, f32[3,64]{1,0:T(4,128)}, u32[]{:S(2)}) copy-start(f32[3,64]{1,0:T(4,128)} %get-tuple-element.193) | copy-start | bytes 2308
  296.8 12.8 %copy-start.56 = (f32[3,64]{1,0:T(4,128)S(1)}, f32[3,64]{1,0:T(4,128)}, u32[]{:S(2)}) copy-start(f32[3,64]{1,0:T(4,128)} %get-tuple-element.191) | copy-start | bytes 2308
  296.9 12.9 %copy-start.38 = (f32[768]{0:T(1024)S(1)}, f32[768]{0:T(1024)}, u32[]{:S(2)}) copy-start(f32[768]{0:T(1024)} %get-tuple-element.175) | copy-start | bytes 9220
  296.9 12.8 %copy-start.39 = (f32[768]{0:T(1024)S(1)}, f32[768]{0:T(1024)}, u32[]{:S(2)}) copy-start(f32[768]{0:T(1024)} %get-tuple-element.142) | copy-start | bytes 9220
  296.9 12.8 %copy-start.40 = (f32[768]{0:T(1024)S(1)}, f32[768]{0:T(1024)}, u32[]{:S(2)}) copy-start(f32[768]{0:T(1024)} %get-tuple-element.147) | copy-start | bytes 9220
  296.9 12.8 %copy-start.49 = (f32[768]{0:T(1024)S(1)}, f32[768]{0:T(1024)}, u32[]{:S(2)}) copy-start(f32[768]{0:T(1024)} %get-tuple-element.140) | copy-start | bytes 9220
  296.9 12.8 %copy-start.50 = (f32[768]{0:T(1024)S(1)}, f32[768]{0:T(1024)}, u32[]{:S(2)}) copy-start(f32[768]{0:T(1024)} %get-tuple-element.146) | copy-start | bytes 9220
  296.9 12.8 %copy-start.51 = (f32[768]{0:T(1024)S(1)}, f32[768]{0:T(1024)}, u32[]{:S(2)}) copy-start(f32[768]{0:T(1024)} %get-tuple-element.219) | copy-start | bytes 9220
  471.1 2.1 copy-start.23
  471.1 2.9 copy-start.22
  471.1 3.7 copy-start.21
  473.2 2.5 copy-start.10
  475.6 2.5 copy-start.9
  475.6 3.9 copy-start.1
  (24 other events, 25.5 us)
Sparse Core Ops, SparseCore 0:
  16.0 71.6 all-reduce.7
  98.5 68.1 all-reduce.9
  188.3 68.1 all-reduce.11
  285.9 68.0 all-reduce.13
  359.1 111.9 all-reduce.15
where the time goes:
time: 487 us; the launch traced here: 486 us
  waiting for transfers between devices  339 us (70%)
  matrix products  55.8 us (11%)
  blocking collectives  35.6 us (7%)
  other arithmetic  20.7 us (4%)
  local copies, waits for them, and re-layouts  19.7 us (4%)
  between operations  14.5 us (3%)
    psum x1, waiting for transfers between devices, shards(): lax.psum((w_query_part, w_key_part, w_value_part, b_query_part, b_value_p...  114 us
    psum x1, waiting for transfers between devices, shards(): attn_total = lax.psum(partial_value, 'tensor')  71.8 us
    psum x1, waiting for transfers between devices, shards(): d_normed = d_resid + lax.psum(normed_term, 'tensor')  68 us
    psum x1, waiting for transfers between devices, shards(): lax.psum(jnp.dot(act_rows, w_down, preferred_element_type=jnp.float32), '...  65.6 us
    psum x1, blocking collectives, shards(): lax.psum((w_query_part, w_key_part, w_value_part, b_query_part, b_value_p...  25 us
    psum x1, waiting for transfers between devices, shards(): d_tokens = d_hidden + lax.psum(input_term, 'tensor')  19.3 us
    unnamed x141, local copies, waits for them, and re-layouts  17.3 us
    all_gather x1, blocking collectives, shards(): lax.all_gather(jnp.concatenate(pieces, axis=1), 'dp', axis=0, tiled=True)  10.6 us
  transfers between devices with their start and end apart: 5, of which 5 were waited for; matrix products, arithmetic and copies ran while one was open for 4% of the time, Pallas kernels for 0%

commit v1 on v0

--- a/solution.py
+++ b/solution.py
@@ -97,7 +97,12 @@
     normed_low = normed.astype(jnp.bfloat16)
     upper = jnp.dot(normed_low, w_up, preferred_element_type=jnp.float32) + b_up
     act_rows = gelu_exact(upper).astype(jnp.bfloat16)
-    down_total = lax.psum(jnp.dot(act_rows, w_down, preferred_element_type=jnp.float32), "tensor")
+
+    def see_cube_up(matrix, link_axis="tensor"):
+        finding = jax.lax.all_gather(matrix, axis_name=link_axis)
+        return jnp.sum(finding, 0)
+
+    down_total = see_cube_up(jnp.dot(act_rows, w_down, preferred_element_type=jnp.float32))
     normal_ffn, inverse_ffn = norm_stats(normed + down_total + b_down)
     final = normal_ffn * g_ffn + b_ffn
     layer_out = final.astype(jnp.bfloat16)

time: 487 us -> 534 us (1.097)
  waiting for transfers between devices: 339 us -> 385 us
    all_gather x0 -> x1, waiting for transfers between devices: none -> 112 us  [see_cube_up(): finding = jax.lax.all_gather(matrix, axis_name=link_axis)]
    psum x1 -> x0, waiting for transfers between devices: 65.6 us -> none  [shards(): lax.psum(jnp.dot(act_rows, w_down, preferred_element_type=jnp.float32), '...]
    unnamed x141 -> x133, local copies, waits for them, and re-layouts: 17.3 us -> 18.4 us
  transfers between devices with their start and end apart: 5 -> 5, of which waited for: 5 -> 5; matrix products, arithmetic and copies ran while one was open for 4% -> 3% of each run, Pallas kernels for 0% -> 0%
where the time goes in v1:
time: 534 us; the launch traced here: 533 us
  waiting for transfers between devices  385 us (72%)
  matrix products  52.8 us (10%)
  blocking collectives  35.6 us (7%)
  other arithmetic  24 us (4%)
  local copies, waits for them, and re-layouts  20.9 us (4%)
  between operations  14.5 us (3%)
    psum x1, waiting for transfers between devices, shards(): lax.psum((w_query_part, w_key_part, w_value_part, b_query_part, b_value_p...  114 us
    all_gather x1, waiting for transfers between devices, see_cube_up(): finding = jax.lax.all_gather(matrix, axis_name=link_axis)  112 us
    psum x1, waiting for transfers between devices, shards(): attn_total = lax.psum(partial_value, 'tensor')  71.8 us
    psum x1, waiting for transfers between devices, shards(): d_normed = d_resid + lax.psum(normed_term, 'tensor')  67 us
    psum x1, blocking collectives, shards(): lax.psum((w_query_part, w_key_part, w_value_part, b_query_part, b_value_p...  25 us
    psum x1, waiting for transfers between devices, shards(): d_tokens = d_hidden + lax.psum(input_term, 'tensor')  19.4 us
    unnamed x133, local copies, waits for them, and re-layouts  18.4 us
  transfers between devices with their start and end apart: 5, of which 5 were waited for; matrix products, arithmetic and copies ran while one was open for 3% of the time, Pallas kernels for 0%

profile of v1, /device:TPU:0, one launch (start us, length us, event | category | flops | bytes accessed | tf_op | source)
XLA Modules:
  0.0 532.9 jit_solution(14862133394301140429)
XLA Ops:
  7.3 0.9 copy.49
  8.6 1.7 convolution_convert_fusion.2
  13.3 1.0 convolution_convert_fusion
  15.0 1.6 fusion.70
  16.6 71.8 %all-reduce.7.cloned.1.call-done = f32[512,768]{1,0:T(8,128)} async-done(((f32[512,768]{1,0:T(8,128)}), f32[512,768]{1,0:T(8,128)}) %all-reduce.7.cloned.1.call-update) | async-done | bytes 1572880 | tf_op jit(solution)/shard_map/psum | solution.py:94
  88.4 1.7 fusion.64
  90.8 5.4 %multiply_convert_fusion.1 = (bf16[512,768]{1,0:T(8,128)(2,1)S(1)}, f32[512,768]{1,0:T(8,128)}, f32[512,768]{1,0:T(8,128)}) fusion(f32[768]{0:T(1024)S(1)} %copy-done.55, bf16[768,768]{1,0:T(8,128)(2,1)S(1)} %copy-done, f32[512,768]{1,0:T(8,128)S(1)} %get-tuple-element.189, f32[768]{0:T(1024)S(1)} %copy-done.51, f32[768]{0:T(1024)S(1)} %copy-done.36, ...), kind=kOutput, calls=%fused_computation.24 | convolution fusion | flops 631898112 | bytes 6697984 | tf_op jit(solution)/shard_map/dot_general | solution.py:98
  96.2 0.9 copy-done.17
  97.1 1.9 fusion.71
  100.6 1.2 convert_bitcast_fusion
  101.7 112.0 %all-gather.3.cloned.1.call-done = f32[2048,768]{1,0:T(8,128)} async-done(((f32[512,768]{1,0:T(8,128)}), f32[2048,768]{1,0:T(8,128)}) %all-gather.3.cloned.1.call-update) | async-done | bytes 6291472 | tf_op jit(solution)/shard_map/all_gather | solution.py:102
  213.7 4.5 reduce_sum.287
  218.2 2.0 fusion.62
  221.2 1.0 multiply_reduce_fusion.9
  225.1 1.3 add_select_fusion.2
  227.1 1.4 scatter-add.19
  228.5 3.9 multiply_reduce_fusion.1
  232.5 1.5 fusion.60
  235.0 1.8 fusion.69
  236.8 0.9 copy-done.59
  237.7 2.0 fusion.42
  240.0 67.0 %all-reduce.9.cloned.1.call-done = f32[512,768]{1,0:T(8,128)} async-done(((f32[512,768]{1,0:T(8,128)}), f32[512,768]{1,0:T(8,128)}) %all-reduce.9.cloned.1.call-update) | async-done | bytes 1572880 | tf_op jit(solution)/shard_map/psum | solution.py:145
  307.0 2.7 multiply_reduce_fusion.2
  311.1 1.2 copy-done.9
  312.3 1.1 fusion.65
  313.4 2.3 fusion.72
  315.7 7.0 %fusion.66 = (f32[3,64]{1,0:T(4,128)S(1)}, bf16[512,3,64]{0,2,1:T(8,128)(2,1)S(1)}) fusion(bf16[512,3,64]{0,2,1:T(8,128)(2,1)S(1)} %bitcast.70, f32[3,512,512]{1,2,0:T(8,128)} %fusion.72, f32[3,512]{1,0:T(4,128)S(1)} %copy-done.42, f32[3,512,512]{1,2,0:T(8,128)} %copy-done.8, pred[512,512]{0,1:T(8,128)(4,1)S(1)} %copy-done.13), kind=kOutput, calls=%fused_computation.151 | convolution fusion | flops 109512512 | bytes 6953728 | tf_op jit(solution)/shard_map/hqk,khd->qhd/dot_general | solution.py:160
  322.7 6.9 %fusion.27 = bf16[3,64,512]{2,1,0:T(8,128)(2,1)S(1)} fusion(bf16[512,3,64]{0,2,1:T(8,128)(2,1)} %bitcast.80, f32[3,512,512]{1,2,0:T(8,128)} %fusion.72, f32[3,512,512]{1,2,0:T(8,128)} %copy-done.8, f32[3,512]{1,0:T(4,128)S(1)} %copy-done.42, pred[512,512]{0,1:T(8,128)(4,1)S(1)} %copy-done.13), kind=kOutput, calls=%fused_computation.60 | convolution fusion | flops 109414400 | bytes 6952960 | tf_op jit(solution)/shard_map/hqk,qhd->khd/dot_general | solution.py:163
  331.0 1.6 add_add_fusion
  332.7 3.9 fusion.44
  336.6 2.4 fusion.40
  339.0 1.1 convolution_bitcast_fusion
  340.2 1.1 convolution_bitcast_fusion.1
  341.3 1.1 convolution_bitcast_fusion.2
  342.5 1.1 fusion.37
  343.7 0.8 copy-done.31
  344.5 10.6 %all_gather.11 = f32[128,1728]{1,0:T(8,128)S(1)} all-gather(f32[16,1728]{1,0:T(8,128)S(1)} %copy-done.31), channel_id=1, replica_groups=mesh['dp'=8,'tensor'=4] {'dp'}, dimensions={0}, use_global_device_ids=true | all-gather | bytes 995328 | tf_op jit(solution)/shard_map/all_gather | solution.py:120
  355.1 1.2 copy.54
  356.5 25.0 %all-reduce = (f32[192]{0:T(256)}, f32[192]{0:T(256)}, f32[768]{0:T(1024)}, f32[768]{0:T(1024)}, f32[768]{0:T(1024)}, /*index=5*/f32[768]{0:T(1024)}, f32[768]{0:T(1024)}, f32[768]{0:T(1024)}, f32[768]{0:T(1024)}) all-reduce(f32[192]{0:T(256)S(1)} %reduce_sum.306, ...), channel_id=1, replica_groups=mesh['dp'=8,'tensor'=4] {'dp'}, use_global_device_ids=true, to_apply=%region_35.36 | all-reduce | flops 5760 | bytes 46080 | tf_op jit(solution)/shard_map/psum | solution.py:185
  381.5 19.4 %all-reduce.11.cloned.1.call-done = f32[512,768]{1,0:T(8,128)} async-done(((f32[512,768]{1,0:T(8,128)}), f32[512,768]{1,0:T(8,128)}) %all-reduce.11.cloned.1.call-update) | async-done | bytes 1572880 | tf_op jit(solution)/shard_map/psum | solution.py:184
  400.9 2.7 add.259
  403.6 114.3 %all-reduce.13.cloned.1.call-done = (f32[768,192]{0,1:T(8,128)}, f32[768,192]{0,1:T(8,128)}, f32[768,192]{0,1:T(8,128)}, f32[192,768]{1,0:T(8,128)}, f32[768,768]{1,0:T(8,128)}, /*index=5*/f32[768,768]{1,0:T(8,128)}) async-done(((f32[768,192]{0,1:T(8,128)}, f32[768,192]{0,1:T(8,128)}, f32[768,192]{0,1:T(8,128)}, f32[192,768]{1,0:T(8,128)}, f32[768,768]{1,0:T(8,128)}, /*index=5*/f32[768,768]{1,0:T(8,128)}), ...) | async-done | bytes 7077904 | tf_op jit(solution)/shard_map/psum | solution.py:185
  517.9 2.0 copy.76
  520.8 0.8 copy.78
  521.6 0.8 copy.79
  522.5 1.4 copy.80
  523.9 1.1 copy-done.10
  525.0 1.4 copy.81
  (172 shorter events, 15.9 us)
Async XLA Ops:
  7.2 83.3 %copy-start = (bf16[768,768]{1,0:T(8,128)(2,1)S(1)}, bf16[768,768]{1,0:T(8,128)(2,1)}, u32[]{:S(2)}) copy-start(bf16[768,768]{1,0:T(8,128)(2,1)} %param.42) | copy-start | bytes 3538948
  7.2 3.1 copy-start.4
  7.2 3.1 copy-start.27
  7.2 3.1 copy-start.56
  7.2 81.2 %all-reduce.7.cloned.1.call-start = ((), (), s32[]{:S(2)}) async-start(), calls=%async_computation | async-start | bytes 3145728 | tf_op jit(solution)/shard_map/psum | solution.py:94
  8.6 4.6 copy-start.12
  11.6 1.7 copy-start.8
  12.8 1.5 copy-start.41
  13.3 1.7 copy-start.15
  15.0 73.4 %copy-start.50 = (f32[768]{0:T(1024)S(1)}, f32[768]{0:T(1024)}, u32[]{:S(2)}) copy-start(f32[768]{0:T(1024)} %param.39) | copy-start | bytes 9220
  16.6 197.1 %all-gather.3.cloned.1.call-start = ((), (), s32[]{:S(2)}) async-start(), calls=%async_computation.3 | async-start | bytes 7864320 | tf_op jit(solution)/shard_map/all_gather | solution.py:102
  90.8 6.3 %copy-start.53 = (bf16[768,768]{1,0:T(8,128)(2,1)S(1)}, bf16[768,768]{1,0:T(8,128)(2,1)}, u32[]{:S(2)}) copy-start(bf16[768,768]{1,0:T(8,128)(2,1)} %param.44) | copy-start | bytes 3538948
  99.0 208.0 %all-reduce.9.cloned.1.call-start = ((), (), s32[]{:S(2)}) async-start(), calls=%async_computation.1 | async-start | bytes 3145728 | tf_op jit(solution)/shard_map/psum | solution.py:145
  220.2 2.1 copy-start.5
  220.2 2.0 copy-start.37
  221.2 5.9 %copy-start.39 = (f32[512]{0:T(512)}, f32[512]{0:T(512)S(1)}, u32[]{:S(2)}) copy-start(f32[512]{0:T(512)S(1)} %add_rsqrt_fusion) | copy-start | bytes 6148
  225.1 2.0 copy-start.35
  228.5 4.0 copy-start.6
  228.5 4.0 copy-start.38
  228.5 4.0 copy-start.40
  228.5 4.0 copy-start.44
  228.5 4.0 copy-start.46
  232.5 1.6 copy-start.54
  232.5 2.0 copy-start.61
  232.5 2.6 copy-start.62
  234.0 2.8 copy-start.7
  239.7 161.2 %all-reduce.11.cloned.1.call-start = ((), (), s32[]{:S(2)}) async-start(), calls=%async_computation.2 | async-start | bytes 3145728 | tf_op jit(solution)/shard_map/psum | solution.py:184
  309.8 2.6 copy-start.9
  310.3 3.1 copy-start.2
  310.3 2.0 copy-start.13
  310.3 2.0 copy-start.42
  313.4 2.3 copy-start.21
  322.7 7.0 %copy-start.14 = (bf16[768,192]{0,1:T(8,128)(2,1)S(1)}, bf16[768,192]{0,1:T(8,128)(2,1)}, u32[]{:S(2)}) copy-start(bf16[768,192]{0,1:T(8,128)(2,1)} %param.34) | copy-start | bytes 884740
  329.7 1.4 copy-start.26
  332.6 4.0 copy-start.52
  332.6 185.3 %all-reduce.13.cloned.1.call-start = ((), (), s32[]{:S(2)}) async-start(), calls=%async_computation.4 | async-start | bytes 14155776 | tf_op jit(solution)/shard_map/psum | solution.py:185
  332.7 3.9 copy-start.60
  340.2 2.3 copy-start.3
  340.2 2.3 copy-start.19
  343.6 12.9 %copy-start.47 = (f32[768]{0:T(1024)S(1)}, f32[768]{0:T(1024)}, u32[]{:S(2)}) copy-start(f32[768]{0:T(1024)} %get-tuple-element.140) | copy-start | bytes 9220
  343.6 12.9 %copy-start.48 = (f32[768]{0:T(1024)S(1)}, f32[768]{0:T(1024)}, u32[]{:S(2)}) copy-start(f32[768]{0:T(1024)} %get-tuple-element.146) | copy-start | bytes 9220
  343.7 12.9 %copy-start.49 = (f32[768]{0:T(1024)S(1)}, f32[768]{0:T(1024)}, u32[]{:S(2)}) copy-start(f32[768]{0:T(1024)} %get-tuple-element.219) | copy-start | bytes 9220
  517.9 2.1 copy-start.24
  517.9 2.9 copy-start.23
  517.9 3.7 copy-start.22
  520.0 2.5 copy-start.11
  522.4 2.5 copy-start.10
  522.5 3.9 copy-start.1
  (20 other events, 18.5 us)
Sparse Core Ops, SparseCore 0:
  16.7 71.6 all-reduce.6
  99.2 114.4 all-gather.2
  239.8 67.1 all-reduce.8
  332.7 68.1 all-reduce.10
  405.9 111.9 all-reduce.12
